TPU v7x, 256 devices: a whole 4x4x8 slice. The times are simulated.
256 devices in a mesh: mp: 16 (over y, x_hi, core), shard: 16 (over z, x_lo).
Axes of the slice: x: 4 (x_hi: 2, x_lo: 2; x = x_hi * 2 + x_lo), y: 4, z: 8, core: 2. Of those that a mesh axis runs over, the one named last changes fastest.
Arguments:
- bank: bfloat16 [4096, 8192], P('shard'), may hold values from -6 to 6
- calib_ids: int32 [16, 1024], P('mp', 'shard'), may hold values from 0 to 4095, as said below
- norm_gains: float32 [16, 8192], P('mp'), may hold values from 0.5 to 1.5
- proj_slabs: bfloat16 [16, 8192, 512], P('mp', 'shard'), may hold values from -0.0625 to 0.0625
Outputs:
- merged_gram: float32 [8192, 8192], P('mp', 'shard')
- numer: float32 [8192, 512], P('shard')
Inputs may be any that keep to these rules, and one draw needn't show every extreme that they name: `calib_ids`: token t of every model names a bank row in block t // 64, rows (t // 64) * 256 to (t // 64) * 256 + 255.
All inputs are finite; a program needn't handle non-finite values.
Results may differ from a plain program's by a relative error of at most 0.0048.
Values may be sent and summed in bfloat16 or wider, within the bound.
No kernel may reach another device: no remote copies, remote signals or barrier semaphores. Data moves between devices by JAX's collectives and lax.ppermute only.
A program may use at most 128 MiB of HBM per device.

v0:
```python
import jax
import jax.numpy as jnp
from jax import lax
from jax.sharding import PartitionSpec as P

ALPHA = 0.9
EPSILON = 1e-05


def local(bank, calib_ids, norm_gains, proj_slabs):
    model_width = bank.shape[1]
    bank_dev = bank.shape[0]
    col_block = model_width // lax.axis_size("shard")
    position = lax.axis_index("shard")
    local_ids = calib_ids[0] - position * bank_dev
    picked = jnp.take(bank, local_ids, axis=0).astype(jnp.float32)
    mean_square = jnp.mean(picked * picked, axis=-1, keepdims=True)
    calib_local = (picked * lax.rsqrt(mean_square + EPSILON) * norm_gains[0][None, :]).astype(
        jnp.bfloat16
    )
    calib = lax.all_gather(calib_local, "shard", axis=0, tiled=True)
    tokens = calib.shape[0]
    own_cols = lax.dynamic_slice_in_dim(calib, position * col_block, col_block, 1)
    own_float = own_cols.astype(jnp.float32)
    diag_part = jnp.sum(own_float * own_float, axis=0) / tokens
    weight_rows = proj_slabs[0]
    partial_out = jnp.dot(own_cols, weight_rows, preferred_element_type=jnp.float32)
    model_out = lax.psum(partial_out, "shard").astype(jnp.bfloat16)
    weighted = lax.dot_general(
        own_cols, model_out, (((0,), (0,)), ((), ())), preferred_element_type=jnp.float32
    )
    numer_part = ALPHA * weighted / tokens + (1.0 - ALPHA) * diag_part[
        :, None
    ] * weight_rows.astype(jnp.float32)
    product = lax.dot_general(
        calib, own_cols, (((0,), (0,)), ((), ())), preferred_element_type=jnp.float32
    )
    product = ALPHA * product / tokens
    row_index = lax.broadcasted_iota(jnp.int32, (model_width, col_block), 0)
    col_index = position * col_block + lax.broadcasted_iota(jnp.int32, (model_width, col_block), 1)
    merged_gram = lax.psum_scatter(
        product + jnp.where(row_index == col_index, (1.0 - ALPHA) * diag_part[None, :], 0.0),
        "mp",
        scatter_dimension=0,
        tiled=True,
    )
    numer = lax.psum(numer_part, "mp")
    return (merged_gram, numer)


def solution(mesh):
    placed = (P("shard", None), P("mp", "shard"), P("mp", None), P("mp", "shard", None))
    return jax.shard_map(
        local,
        mesh=mesh,
        in_specs=placed,
        out_specs=(P("mp", "shard"), P("shard", None)),
        check_vma=False,
    )
```

profile of v0, /device:TPU:1, one launch (start us, length us, event | category | flops | bytes accessed | tf_op | source)
XLA Modules:
  0.0 796.7 jit_solution(8639390773371479828)
XLA Ops:
  7.2 0.0 all-gather.2.cloned.1.call-start
  7.2 0.7 fusion.10
  7.9 0.7 compare_and_fusion
  8.5 4.9 gather_fusion
  13.4 0.5 fusion
  13.9 2.1 fusion.2
  16.0 0.0 all-gather.2.cloned.1.call-update
  16.0 0.0 all-reduce.3.cloned.1.call-start
  16.1 354.9 %all-gather.2.cloned.1.call-done = bf16[1024,8192]{1,0:T(8,128)(2,1)} async-done(((bf16[64,8192]{1,0:T(8,128)(2,1)}), bf16[1024,8192]{1,0:T(8,128)(2,1)}) %all-gather.2.cloned.1.call-update) | async-done | bytes 16777232 | tf_op jit(solution)/shard_map/all_gather | solution.py:21
  371.0 1.5 multiply_reduce_fusion
  372.5 2.1 fusion.6
  374.5 94.7 %all-reduce.4 = bf16[1024,512]{1,0:T(8,128)(2,1)S(1)} all-reduce(f32[1024,512]{1,0:T(8,128)S(1)} %fusion.6), channel_id=1, replica_groups=mesh['mp'=16,'shard'=16] {'shard'}, use_global_device_ids=true, to_apply=%region_3.4 | all-reduce | flops 524288 | bytes 3145728 | tf_op jit(solution)/shard_map/psum | solution.py:28
  469.3 3.1 fusion.3
  472.4 0.0 all-reduce.3.cloned.1.call-update
  472.4 0.0 reduce-scatter.2.cloned.1.call-start
  472.4 17.9 %select_add_fusion = f32[8192,512]{1,0:T(8,128)} fusion(bf16[1024,8192]{1,0:T(8,128)(2,1)} %all-gather.2.cloned.1.call-done, f32[512]{0:T(512)S(1)} %broadcast_multiply_fusion, s32[512]{0:T(512)S(1)} %iota_add_fusion, s32[]{:T(128)S(6)} %select_n.30), kind=kOutput, calls=%fused_computation.1 | convolution fusion | flops 8606711808 | bytes 34607108 | tf_op jit(solution)/shard_map/dot_general | solution.py:35
  490.3 0.0 reduce-scatter.2.cloned.1.call-update
  490.4 135.9 %all-reduce.3.cloned.1.call-done = f32[512,512]{1,0:T(8,128)} async-done(((f32[512,512]{1,0:T(8,128)}), f32[512,512]{1,0:T(8,128)}) %all-reduce.3.cloned.1.call-update) | async-done | bytes 1048592 | tf_op jit(solution)/shard_map/psum | solution.py:47
  626.2 161.7 %reduce-scatter.2.cloned.1.call-done = f32[512,512]{1,0:T(8,128)} async-done(((f32[8192,512]{1,0:T(8,128)}), f32[512,512]{1,0:T(8,128)}) %reduce-scatter.2.cloned.1.call-update) | async-done | bytes 1048592 | tf_op jit(solution)/shard_map/reduce_scatter | solution.py:41
  787.9 2.3 copy.9
  (4 shorter events, 0.0 us)
Async XLA Ops:
  7.2 363.8 %all-gather.2.cloned.1.call-start = ((), (), s32[]{:S(2)}) async-start(), calls=%async_computation.1 | async-start | bytes 17825792 | tf_op jit(solution)/shard_map/all_gather | solution.py:21
  16.0 610.2 %all-reduce.3.cloned.1.call-start = ((), (), s32[]{:S(2)}) async-start(), calls=%async_computation.3 | async-start | bytes 2097152 | tf_op jit(solution)/shard_map/psum | solution.py:47
  472.4 315.6 %reduce-scatter.2.cloned.1.call-start = ((), (), s32[]{:S(2)}) async-start(), calls=%async_computation.2 | async-start | bytes 17825792 | tf_op jit(solution)/shard_map/reduce_scatter | solution.py:41
Sparse Core Ops, SparseCore 0:
  16.2 354.7 all-gather.1
  472.5 153.6 all-reduce.2
  632.1 155.7 reduce-scatter.1
where the time goes:
time: 797 us
  waiting for transfers between devices  652 us (82%)
  blocking collectives  94.7 us (12%)
  matrix products  23 us (3%)
  between operations  13.8 us (2%)
    all_gather x1, waiting for transfers between devices, local(): calib = lax.all_gather(calib_local, 'shard', axis=0, tiled=True)  355 us
    reduce_scatter x1, waiting for transfers between devices, local(): lax.psum_scatter(product + jnp.where(row_index == col_index, (1.0 - ALPHA...  162 us
    psum x1, waiting for transfers between devices, local(): numer = lax.psum(numer_part, 'mp')  136 us
    psum x1, blocking collectives, local(): model_out = lax.psum(partial_out, 'shard').astype(jnp.bfloat16)  94.7 us
    dot_general x1, matrix products, local(): lax.dot_general(calib, own_cols, (((0,), (0,)), ((), ())), preferred_elem...  17.9 us
  transfers between devices with their start and end apart: 3, of which 3 were waited for; matrix products, arithmetic and copies ran while one was open for 2% of the time, Pallas kernels for 0%

commit v1 on v0

--- a/solution.py
+++ b/solution.py
@@ -44,7 +44,7 @@
         scatter_dimension=0,
         tiled=True,
     )
-    numer = lax.psum(numer_part, "mp")
+    numer = jnp.sum(lax.all_gather(numer_part, "mp"), axis=0)
     return (merged_gram, numer)
 
 

time: 797 us -> 760 us (0.954)
  waiting for transfers between devices: 652 us -> 608 us
  other arithmetic: 5.41 us -> 14.3 us
    psum x1 -> x0, waiting for transfers between devices: 136 us -> none  [local(): numer = lax.psum(numer_part, 'mp')]
    all_gather x0 -> x1, waiting for transfers between devices: none -> 106 us  [local(): numer = jnp.sum(lax.all_gather(numer_part, 'mp'), axis=0)]
    reduce_scatter x1, waiting for transfers between devices: 162 us -> 148 us  [local(): lax.psum_scatter(product + jnp.where(row_index == col_index, (1.0 - ALPHA...]
    reduce_sum x0 -> x1, other arithmetic: none -> 8.88 us  [local(): numer = jnp.sum(lax.all_gather(numer_part, 'mp'), axis=0)]
  transfers between devices with their start and end apart: 3 -> 3, of which waited for: 3 -> 3; matrix products, arithmetic and copies ran while one was open for 2% -> 4% of each run, Pallas kernels for 0% -> 0%
where the time goes in v1:
time: 760 us; the launch traced here: 759 us
  waiting for transfers between devices  608 us (80%)
  blocking collectives  94.5 us (12%)
  matrix products  23 us (3%)
  other arithmetic  14.3 us (2%)
  between operations  13.8 us (2%)
    all_gather x1, waiting for transfers between devices, local(): calib = lax.all_gather(calib_local, 'shard', axis=0, tiled=True)  355 us
    reduce_scatter x1, waiting for transfers between devices, local(): lax.psum_scatter(product + jnp.where(row_index == col_index, (1.0 - ALPHA...  148 us
    all_gather x1, waiting for transfers between devices, local(): numer = jnp.sum(lax.all_gather(numer_part, 'mp'), axis=0)  106 us
    psum x1, blocking collectives, local(): model_out = lax.psum(partial_out, 'shard').astype(jnp.bfloat16)  94.5 us
    dot_general x1, matrix products, local(): lax.dot_general(calib, own_cols, (((0,), (0,)), ((), ())), preferred_elem...  17.9 us
  transfers between devices with their start and end apart: 3, of which 3 were waited for; matrix products, arithmetic and copies ran while one was open for 4% of the time, Pallas kernels for 0%

profile of v1, /device:TPU:1, one launch (start us, length us, event | category | flops | bytes accessed | tf_op | source)
XLA Modules:
  0.0 759.2 jit_solution(2730780854549361860)
XLA Ops:
  7.2 0.0 all-gather.4.cloned.1.call-start
  7.2 0.7 fusion.10
  7.9 0.7 compare_and_fusion
  8.5 4.9 gather_fusion
  13.4 0.5 fusion
  13.9 2.1 fusion.2
  16.0 0.0 all-gather.4.cloned.1.call-update
  16.0 0.0 all-gather.6.cloned.1.call-start
  16.1 354.9 %all-gather.4.cloned.1.call-done = bf16[1024,8192]{1,0:T(8,128)(2,1)} async-done(((bf16[64,8192]{1,0:T(8,128)(2,1)}), bf16[1024,8192]{1,0:T(8,128)(2,1)}) %all-gather.4.cloned.1.call-update) | async-done | bytes 16777232 | tf_op jit(solution)/shard_map/all_gather | solution.py:21
  371.0 1.5 multiply_reduce_fusion
  372.5 2.1 fusion.6
  374.5 94.5 %all-reduce.1 = bf16[1024,512]{1,0:T(8,128)(2,1)S(1)} all-reduce(f32[1024,512]{1,0:T(8,128)S(1)} %fusion.6), channel_id=1, replica_groups=mesh['mp'=16,'shard'=16] {'shard'}, use_global_device_ids=true, to_apply=%region_3.4 | all-reduce | flops 524288 | bytes 3145728 | tf_op jit(solution)/shard_map/psum | solution.py:28
  469.1 3.1 fusion.3
  472.2 0.0 all-gather.6.cloned.1.call-update
  472.2 0.2 reduce-scatter.2.cloned.1.call-start
  472.4 17.9 %select_add_fusion = f32[8192,512]{1,0:T(8,128)} fusion(bf16[1024,8192]{1,0:T(8,128)(2,1)} %all-gather.4.cloned.1.call-done, f32[512]{0:T(512)S(1)} %broadcast_multiply_fusion, s32[512]{0:T(512)S(1)} %iota_add_fusion, s32[]{:T(128)S(6)} %select_n.30), kind=kOutput, calls=%fused_computation.1 | convolution fusion | flops 8606711808 | bytes 34607108 | tf_op jit(solution)/shard_map/dot_general | solution.py:35
  490.3 0.0 reduce-scatter.2.cloned.1.call-update
  490.3 105.5 %all-gather.6.cloned.1.call-done = f32[8192,512]{1,0:T(8,128)} async-done(((f32[512,512]{1,0:T(8,128)}), f32[8192,512]{1,0:T(8,128)}) %all-gather.6.cloned.1.call-update) | async-done | bytes 16777232 | tf_op jit(solution)/shard_map/all_gather | solution.py:47
  595.8 8.9 %reduce_sum.29 = f32[512,512]{1,0:T(8,128)} reduce(f32[16,512,512]{2,1,0:T(8,128)} %bitcast.14, f32[]{:T(128)} %constant.20.clone.1), dimensions={0}, to_apply=%region_4.5 | reduce | flops 3932160 | bytes 17825796 | tf_op jit(solution)/shard_map/reduce_sum | solution.py:47
  604.7 148.0 %reduce-scatter.2.cloned.1.call-done = f32[512,512]{1,0:T(8,128)} async-done(((f32[8192,512]{1,0:T(8,128)}), f32[512,512]{1,0:T(8,128)}) %reduce-scatter.2.cloned.1.call-update) | async-done | bytes 1048592 | tf_op jit(solution)/shard_map/reduce_scatter | solution.py:41
  (4 shorter events, 0.0 us)
Async XLA Ops:
  7.2 363.8 %all-gather.4.cloned.1.call-start = ((), (), s32[]{:S(2)}) async-start(), calls=%async_computation.1 | async-start | bytes 17825792 | tf_op jit(solution)/shard_map/all_gather | solution.py:21
  16.0 579.8 %all-gather.6.cloned.1.call-start = ((), (), s32[]{:S(2)}) async-start(), calls=%async_computation.3 | async-start | bytes 17825792 | tf_op jit(solution)/shard_map/all_gather | solution.py:47
  472.2 280.5 %reduce-scatter.2.cloned.1.call-start = ((), (), s32[]{:S(2)}) async-start(), calls=%async_computation.2 | async-start | bytes 17825792 | tf_op jit(solution)/shard_map/reduce_scatter | solution.py:41
Sparse Core Ops, SparseCore 0:
  16.2 354.7 all-gather.3
  472.3 123.4 all-gather.5
  601.0 151.6 reduce-scatter.1
